TPU v7x, 128 devices: a whole 4x4x4 slice. The times are simulated.
128 devices in a mesh: wide: 32 (over x, z, core), narrow: 4 (over y).
Axes of the slice: x: 4, y: 4, z: 4, core: 2. Of those that a mesh axis runs over, the one named last changes fastest.
Arguments:
- tokens: bfloat16 [262144, 1024], P(('wide', 'narrow')), may hold values from -64 to 64
- slot_params: bfloat16 [1024, 512], replicated, may hold values from -2.5 to 2.5
- expert_in: bfloat16 [128, 1024, 4096], P('wide', None, 'narrow'), may hold values from -0.1875 to 0.1875
- expert_out: bfloat16 [128, 4096, 1024], P('wide', 'narrow'), may hold values from -0.09375 to 0.09375
Outputs:
- mixed: bfloat16 [262144, 1024], P(('wide', 'narrow'))
All inputs are finite; a program needn't handle non-finite values.
Results may differ from a plain program's by a relative error of at most 0.0071.
Values may be sent and summed in bfloat16 or wider, within the bound.
A program may use at most 128 MiB of HBM per device.

v0:
```python
import jax
import jax.numpy as jnp
from jax import lax
from jax.sharding import PartitionSpec as P

SLOT_PER = 4


def divide_rows(summed, slot_totals):
    return (summed / slot_totals[:, None]).astype(jnp.bfloat16)


def shards(tokens, slot_params, expert_in, expert_out):
    logits = jnp.dot(tokens, slot_params, preferred_element_type=jnp.float32)
    local_peak = jnp.max(logits, axis=0)
    column_peak = lax.pmax(local_peak, ("wide", "narrow"))
    weights = jnp.exp(logits - column_peak)
    slot_totals = lax.psum(jnp.sum(weights, axis=0), ("wide", "narrow"))
    dispatch = weights.astype(jnp.bfloat16)
    slot_count = slot_params.shape[1]
    row_count = slot_count // lax.axis_size("wide")
    columns = dispatch
    partial_value = lax.psum_scatter(
        lax.dot_general(
            columns, tokens, (((0,), (0,)), ((), ())), preferred_element_type=jnp.float32
        ),
        "wide",
        scatter_dimension=0,
        tiled=True,
    )
    summed = lax.psum(partial_value, "narrow")
    owned_totals = lax.dynamic_slice_in_dim(
        slot_totals, lax.axis_index("wide") * row_count, row_count
    )
    slot_in = divide_rows(summed, owned_totals)
    slot_stack = slot_in.reshape(expert_in.shape[0], SLOT_PER, slot_in.shape[1])
    hidden = jax.nn.gelu(
        jnp.einsum("esd,edh->esh", slot_stack, expert_in, preferred_element_type=jnp.float32)
    ).astype(jnp.bfloat16)
    expert_sum = jnp.einsum("esh,ehd->esd", hidden, expert_out, preferred_element_type=jnp.float32)
    expert_sum = expert_sum.reshape(-1, expert_sum.shape[2])
    mixing = jax.nn.softmax(logits, axis=1).astype(jnp.bfloat16)
    whole_rows = lax.psum(expert_sum, "narrow").astype(jnp.bfloat16)
    columns = mixing
    mixed = jnp.dot(
        columns,
        lax.all_gather(whole_rows, "wide", axis=0, tiled=True),
        preferred_element_type=jnp.float32,
    )
    return mixed.astype(jnp.bfloat16)


def solution(mesh):
    return jax.shard_map(
        shards,
        mesh=mesh,
        in_specs=(
            P(("wide", "narrow"), None),
            P(),
            P("wide", None, "narrow"),
            P("wide", "narrow", None),
        ),
        out_specs=P(("wide", "narrow"), None),
        check_vma=False,
    )
```

profile of v0, /device:TPU:1, one launch (start us, length us, event | category | flops | bytes accessed | tf_op | source)
XLA Modules:
  0.0 312.3 jit_solution(13459068889585292751)
XLA Ops:
  6.5 0.0 copy-start
  6.5 0.0 reduce-scatter.2.cloned.1.call-start
  6.5 1.2 copy-done
  7.8 6.5 %fusion.26 = (f32[2048]{0:T(1024)S(1)}, f32[512]{0:T(512)S(1)}, f32[2048,512]{1,0:T(8,128)}) fusion(bf16[2048,1024]{1,0:T(8,128)(2,1)} %param.4, bf16[1024,512]{1,0:T(8,128)(2,1)S(1)} %copy-done), kind=kOutput, calls=%fused_computation.30 | convolution fusion | flops 2149578240 | bytes 9447424 | tf_op jit(solution)/shard_map/dot_general | solution.py:14
  14.2 68.6 %pmax.7 = f32[512]{0:T(512)S(1)} all-reduce(f32[512]{0:T(512)S(1)} %get-tuple-element.8), channel_id=1, replica_groups=mesh['wide'=32,'narrow'=4] {'wide','narrow'}, use_global_device_ids=true, to_apply=%region_3.0 | all-reduce | flops 512 | bytes 4096 | tf_op jit(solution)/shard_map/pmax | solution.py:16
  82.8 7.2 %fusion.3 = f32[512,1024]{1,0:T(8,128)} fusion(bf16[2048,1024]{1,0:T(8,128)(2,1)} %param.4, f32[2048,512]{1,0:T(8,128)} %get-tuple-element.9, f32[512]{0:T(512)S(1)} %pmax.7), kind=kOutput, calls=%fused_computation.7 | convolution fusion | flops 2149580800 | bytes 10487808 | tf_op jit(solution)/shard_map/dot_general | solution.py:24
  90.0 0.0 reduce-scatter.2.cloned.1.call-update
  90.0 0.0 all-reduce.2.cloned.1.call-start
  90.1 73.9 %reduce-scatter.2.cloned.1.call-done = f32[16,1024]{1,0:T(8,128)} async-done(((f32[512,1024]{1,0:T(8,128)}), f32[16,1024]{1,0:T(8,128)}) %reduce-scatter.2.cloned.1.call-update) | async-done | bytes 65552 | tf_op jit(solution)/shard_map/reduce_scatter | solution.py:23
  163.9 0.0 all-reduce.2.cloned.1.call-update
  164.0 0.0 all-gather.2.cloned.1.call-start
  164.0 3.1 %fusion = (f32[2048]{0:T(1024)S(1)}, f32[512]{0:T(512)S(1)}) fusion(f32[2048,512]{1,0:T(8,128)} %get-tuple-element.9, f32[2048]{0:T(1024)S(1)} %get-tuple-element.7, f32[512]{0:T(512)S(1)} %pmax.7), kind=kLoop, calls=%fused_computation.4 | loop fusion | flops 4191744 | bytes 4214784 | tf_op jit(solution)/shard_map/reduce_sum | solution.py:42
  167.2 66.0 %psum.22 = f32[512]{0:T(512)S(1)} all-reduce(f32[512]{0:T(512)S(1)} %get-tuple-element.6), channel_id=1, replica_groups=mesh['wide'=32,'narrow'=4] {'wide','narrow'}, use_global_device_ids=true, to_apply=%region_7.0 | all-reduce | flops 512 | bytes 4096 | tf_op jit(solution)/shard_map/psum | solution.py:18
  233.2 0.1 dynamic_slice.3
  233.3 0.0 all-reduce.2.cloned.1.call-done
  233.3 0.9 divide_convert_fusion.2
  234.2 8.0 %fusion.16 = f32[4,4,1024]{2,1,0:T(4,128)S(1)} fusion(bf16[4,1024,1024]{2,1,0:T(8,128)(2,1)} %param.7, bf16[4,4,1024]{2,1,0:T(4,128)(2,1)S(1)} %reshape.10, bf16[4,1024,1024]{2,1,0:T(8,128)(2,1)} %param.6), kind=kOutput, calls=%fused_computation.21 | convolution fusion | flops 67256320 | bytes 16875520 | tf_op jit(solution)/shard_map/esh,ehd->esd/dot_general | solution.py:40
  242.3 12.6 %psum.23 = bf16[16,1024]{1,0:T(8,128)(2,1)} all-reduce(f32[16,1024]{1,0:T(8,128)S(1)} %reshape.11), channel_id=1, replica_groups=mesh['wide'=32,'narrow'=4] {'narrow'}, use_global_device_ids=true, to_apply=%region_8.0 | all-reduce | flops 16384 | bytes 98304 | tf_op jit(solution)/shard_map/psum | solution.py:43
  254.9 0.0 all-gather.2.cloned.1.call-update
  254.9 43.9 %all-gather.2.cloned.1.call-done = bf16[512,1024]{1,0:T(8,128)(2,1)} async-done(((bf16[16,1024]{1,0:T(8,128)(2,1)}), bf16[512,1024]{1,0:T(8,128)(2,1)}) %all-gather.2.cloned.1.call-update) | async-done | bytes 1048592 | tf_op jit(solution)/shard_map/all_gather | solution.py:47
  298.7 7.0 %convolution_convert_fusion = bf16[2048,1024]{1,0:T(8,128)(2,1)} fusion(bf16[512,1024]{1,0:T(8,128)(2,1)} %all-gather.2.cloned.1.call-done, f32[2048,512]{1,0:T(8,128)} %get-tuple-element.9, f32[2048]{0:T(1024)S(1)} %get-tuple-element.5, f32[2048]{0:T(1024)S(1)} %get-tuple-element.7), kind=kOutput, calls=%fused_computation.3 | convolution fusion | flops 2152726528 | bytes 9453568 | tf_op jit(solution)/shard_map/dot_general | solution.py:45
  (2 shorter events, 0.1 us)
Async XLA Ops:
  6.5 1.2 copy-start
  6.5 157.4 %reduce-scatter.2.cloned.1.call-start = ((), (), s32[]{:S(2)}) async-start(), calls=%async_computation.1 | async-start | bytes 2162688 | tf_op jit(solution)/shard_map/reduce_scatter | solution.py:23
  90.0 143.2 %all-reduce.2.cloned.1.call-start = ((), (), s32[]{:S(2)}) async-start(), calls=%async_computation.2 | async-start | bytes 131072 | tf_op jit(solution)/shard_map/psum | solution.py:31
  164.0 134.8 %all-gather.2.cloned.1.call-start = ((), (), s32[]{:S(2)}) async-start(), calls=%async_computation.3 | async-start | bytes 1081344 | tf_op jit(solution)/shard_map/all_gather | solution.py:47
Sparse Core Ops, SparseCore 0:
  90.2 73.7 reduce-scatter.1
  166.2 40.1 all-reduce.1
  255.0 43.6 all-gather.1
where the time goes:
time: 313 us; the launch traced here: 312 us
  blocking collectives  147 us (47%)
  waiting for transfers between devices  118 us (38%)
  matrix products  28.7 us (9%)
  between operations  13.1 us (4%)
  other arithmetic  4.06 us (1%)
    reduce_scatter x1, waiting for transfers between devices, shards(): lax.psum_scatter(lax.dot_general(columns, tokens, (((0,), (0,)), ((), ())...  73.9 us
    pmax x1, blocking collectives, shards(): column_peak = lax.pmax(local_peak, ('wide', 'narrow'))  68.6 us
    psum x1, blocking collectives, shards(): slot_totals = lax.psum(jnp.sum(weights, axis=0), ('wide', 'narrow'))  66 us
    all_gather x1, waiting for transfers between devices, shards(): lax.all_gather(whole_rows, 'wide', axis=0, tiled=True)  43.9 us
    psum x1, blocking collectives, shards(): whole_rows = lax.psum(expert_sum, 'narrow').astype(jnp.bfloat16)  12.6 us
    dot_general x1, matrix products, shards(): jnp.einsum('esh,ehd->esd', hidden, expert_out, preferred_element_type=jnp...  8.04 us
    dot_general x1, matrix products, shards(): lax.dot_general(columns, tokens, (((0,), (0,)), ((), ())), preferred_elem...  7.15 us
    dot_general x1, matrix products, shards(): jnp.dot(columns, lax.all_gather(whole_rows, 'wide', axis=0, tiled=True),...  7.05 us
  transfers between devices with their start and end apart: 3, of which 2 were waited for; matrix products, arithmetic and copies ran while one was open for 1% of the time, Pallas kernels for 0%

commit v1 on v0

--- a/solution.py
+++ b/solution.py
@@ -4,6 +4,11 @@
 from jax.sharding import PartitionSpec as P
 
 SLOT_PER = 4
+
+
+def gather_from_all(shard, axis, dim):
+    copies = jnp.concatenate([shard] * lax.axis_size(axis), axis=dim)
+    return lax.all_to_all(copies, axis, dim, dim, tiled=True)
 
 
 def divide_rows(summed, slot_totals):
@@ -43,9 +48,7 @@
     whole_rows = lax.psum(expert_sum, "narrow").astype(jnp.bfloat16)
     columns = mixing
     mixed = jnp.dot(
-        columns,
-        lax.all_gather(whole_rows, "wide", axis=0, tiled=True),
-        preferred_element_type=jnp.float32,
+        columns, gather_from_all(whole_rows, "wide", 0), preferred_element_type=jnp.float32
     )
     return mixed.astype(jnp.bfloat16)
 

time: 313 us -> 292 us (0.933)
  waiting for transfers between devices: 118 us -> 73.9 us
  blocking collectives: 147 us -> 172 us
    all_gather x1 -> x0, waiting for transfers between devices: 43.9 us -> none  [shards(): lax.all_gather(whole_rows, 'wide', axis=0, tiled=True)]
    all_to_all x0 -> x1, blocking collectives: none -> 25.7 us  [gather_from_all(): return lax.all_to_all(copies, axis, dim, dim, tiled=True)]
  transfers between devices with their start and end apart: 3 -> 2, of which waited for: 2 -> 1; matrix products, arithmetic and copies ran while one was open for 1% -> 1% of each run, Pallas kernels for 0% -> 0%
where the time goes in v1:
time: 292 us; the launch traced here: 291 us
  blocking collectives  172 us (59%)
  waiting for transfers between devices  73.9 us (25%)
  matrix products  25.9 us (9%)
  between operations  13.7 us (5%)
  other arithmetic  4.06 us (1%)
    reduce_scatter x1, waiting for transfers between devices, shards(): lax.psum_scatter(lax.dot_general(columns, tokens, (((0,), (0,)), ((), ())...  73.9 us
    pmax x1, blocking collectives, shards(): column_peak = lax.pmax(local_peak, ('wide', 'narrow'))  68.6 us
    psum x1, blocking collectives, shards(): slot_totals = lax.psum(jnp.sum(weights, axis=0), ('wide', 'narrow'))  66 us
    all_to_all x1, blocking collectives, gather_from_all(): return lax.all_to_all(copies, axis, dim, dim, tiled=True)  25.7 us
    psum x1, blocking collectives, shards(): whole_rows = lax.psum(expert_sum, 'narrow').astype(jnp.bfloat16)  11.8 us
    dot_general x1, matrix products, shards(): jnp.einsum('esh,ehd->esd', hidden, expert_out, preferred_element_type=jnp...  8.04 us
    dot_general x1, matrix products, shards(): lax.dot_general(columns, tokens, (((0,), (0,)), ((), ())), preferred_elem...  7.19 us
    dot_general x1, matrix products, shards(): logits = jnp.dot(tokens, slot_params, preferred_element_type=jnp.float32)  6.55 us
  transfers between devices with their start and end apart: 2, of which 1 were waited for; matrix products, arithmetic and copies ran while one was open for 1% of the time, Pallas kernels for 0%

profile of v1, /device:TPU:1, one launch (start us, length us, event | category | flops | bytes accessed | tf_op | source)
XLA Modules:
  0.0 291.1 jit_solution(18299405933131504033)
XLA Ops:
  6.5 0.0 copy-start
  6.5 0.0 reduce-scatter.2.cloned.1.call-start
  6.5 1.2 copy-done
  7.8 6.5 %fusion.26 = (f32[2048]{0:T(1024)S(1)}, f32[512]{0:T(512)S(1)}, f32[2048,512]{1,0:T(8,128)}) fusion(bf16[2048,1024]{1,0:T(8,128)(2,1)} %param.4, bf16[1024,512]{1,0:T(8,128)(2,1)S(1)} %copy-done), kind=kOutput, calls=%fused_computation.62 | convolution fusion | flops 2149578240 | bytes 9447424 | tf_op jit(solution)/shard_map/dot_general | solution.py:19
  14.3 68.6 %pmax.7 = f32[512]{0:T(512)S(1)} all-reduce(f32[512]{0:T(512)S(1)} %get-tuple-element.8), channel_id=1, replica_groups=mesh['wide'=32,'narrow'=4] {'wide','narrow'}, use_global_device_ids=true, to_apply=%region_3.0 | all-reduce | flops 512 | bytes 4096 | tf_op jit(solution)/shard_map/pmax | solution.py:21
  82.9 7.2 %fusion.3 = f32[512,1024]{1,0:T(8,128)} fusion(bf16[2048,1024]{1,0:T(8,128)(2,1)} %param.4, f32[2048,512]{1,0:T(8,128)} %get-tuple-element.9, f32[512]{0:T(512)S(1)} %pmax.7), kind=kOutput, calls=%fused_computation.7 | convolution fusion | flops 2149580800 | bytes 10487808 | tf_op jit(solution)/shard_map/dot_general | solution.py:29
  90.1 0.0 reduce-scatter.2.cloned.1.call-update
  90.2 0.0 all-reduce.2.cloned.1.call-start
  90.2 73.9 %reduce-scatter.2.cloned.1.call-done = f32[16,1024]{1,0:T(8,128)} async-done(((f32[512,1024]{1,0:T(8,128)}), f32[16,1024]{1,0:T(8,128)}) %reduce-scatter.2.cloned.1.call-update) | async-done | bytes 65552 | tf_op jit(solution)/shard_map/reduce_scatter | solution.py:28
  164.1 0.0 all-reduce.2.cloned.1.call-update
  164.1 3.1 %fusion = (f32[2048]{0:T(1024)S(1)}, f32[512]{0:T(512)S(1)}) fusion(f32[2048,512]{1,0:T(8,128)} %get-tuple-element.9, f32[2048]{0:T(1024)S(1)} %get-tuple-element.7, f32[512]{0:T(512)S(1)} %pmax.7), kind=kLoop, calls=%fused_computation.4 | loop fusion | flops 4191744 | bytes 4214784 | tf_op jit(solution)/shard_map/reduce_sum | solution.py:47
  167.3 66.0 %psum.22 = f32[512]{0:T(512)S(1)} all-reduce(f32[512]{0:T(512)S(1)} %get-tuple-element.6), channel_id=1, replica_groups=mesh['wide'=32,'narrow'=4] {'wide','narrow'}, use_global_device_ids=true, to_apply=%region_7.0 | all-reduce | flops 512 | bytes 4096 | tf_op jit(solution)/shard_map/psum | solution.py:23
  233.2 0.1 dynamic_slice.3
  233.3 0.0 all-reduce.2.cloned.1.call-done
  233.3 0.9 divide_convert_fusion.2
  234.3 8.0 %fusion.16 = f32[4,4,1024]{2,1,0:T(4,128)S(1)} fusion(bf16[4,1024,1024]{2,1,0:T(8,128)(2,1)} %param.7, bf16[4,4,1024]{2,1,0:T(4,128)(2,1)S(1)} %reshape.12, bf16[4,1024,1024]{2,1,0:T(8,128)(2,1)} %param.6), kind=kOutput, calls=%fused_computation.53 | convolution fusion | flops 67256320 | bytes 16875520 | tf_op jit(solution)/shard_map/esh,ehd->esd/dot_general | solution.py:45
  242.3 11.8 %psum.23 = bf16[16,1024]{1,0:T(8,128)(2,1)S(1)} all-reduce(f32[16,1024]{1,0:T(8,128)S(1)} %reshape.13), channel_id=1, replica_groups=mesh['wide'=32,'narrow'=4] {'narrow'}, use_global_device_ids=true, to_apply=%region_8.0 | all-reduce | flops 16384 | bytes 98304 | tf_op jit(solution)/shard_map/psum | solution.py:48
  254.1 0.0 copy-start.1
  254.5 25.7 %all_to_all.12 = bf16[32,16,1024]{2,1,0:T(8,128)(2,1)S(1)} all-to-all(bf16[32,16,1024]{2,1,0:T(8,128)(2,1)S(1)} %bitcast.9), channel_id=1, replica_groups=mesh['wide'=32,'narrow'=4] {'wide'}, dimensions={0} | all-to-all | bytes 2097152 | tf_op jit(solution)/shard_map/all_to_all | solution.py:11
  280.2 0.0 copy-done.1
  280.2 4.1 %convolution_convert_fusion = bf16[2048,1024]{1,0:T(8,128)(2,1)} fusion(bf16[512,1024]{1,0:T(8,128)(2,1)S(1)} %bitcast.10, f32[2048,512]{1,0:T(8,128)S(1)} %copy-done.1, f32[2048]{0:T(1024)S(1)} %get-tuple-element.5, f32[2048]{0:T(1024)S(1)} %get-tuple-element.7), kind=kOutput, calls=%fused_computation.3 | convolution fusion | flops 2152726528 | bytes 9453568 | tf_op jit(solution)/shard_map/dot_general | solution.py:50
  (34 shorter events, 0.2 us)
Async XLA Ops:
  6.5 1.2 copy-start
  6.5 157.6 %reduce-scatter.2.cloned.1.call-start = ((), (), s32[]{:S(2)}) async-start(), calls=%async_computation.2 | async-start | bytes 2162688 | tf_op jit(solution)/shard_map/reduce_scatter | solution.py:28
  90.2 143.2 %all-reduce.2.cloned.1.call-start = ((), (), s32[]{:S(2)}) async-start(), calls=%async_computation.3 | async-start | bytes 131072 | tf_op jit(solution)/shard_map/psum | solution.py:36
  254.1 26.1 %copy-start.1 = (f32[2048,512]{1,0:T(8,128)S(1)}, f32[2048,512]{1,0:T(8,128)}, u32[]{:S(2)}) copy-start(f32[2048,512]{1,0:T(8,128)} %get-tuple-element.9) | copy-start | bytes 12582916
Sparse Core Ops, SparseCore 0:
  90.3 73.7 reduce-scatter.1
  166.4 40.0 all-reduce.1
